TPU v7x, 32 devices: a whole 2x2x4 slice. The times are simulated.
32 devices in a mesh: groups: 2 (over x), expert: 2 (over core), seq: 8 (over z, y).
Axes of the slice: x: 2, y: 2, z: 4, core: 2. Of those that a mesh axis runs over, the one named last changes fastest.
Arguments:
- query_heads: bfloat16 [2, 2, 2080, 4096], P('expert', 'groups', 'seq'), parts along dimension 1, may hold values from -100 to 100
- key_heads: bfloat16 [2, 2, 2080, 4096], P('expert', 'groups', 'seq'), parts along dimension 1, may hold values from -8 to 8
- value_heads: bfloat16 [2, 2, 2080, 4096], P('expert', 'groups', 'seq'), parts along dimension 1, may hold values from -6 to 6
- residual: bfloat16 [2, 2, 2080, 5120], P('expert', 'groups', 'seq'), parts along dimension 1, may hold values from -6 to 6
- out_weight: bfloat16 [2, 4096, 5120], P('expert', 'seq'), may hold values from -0.09375 to 0.09375
- mod_weight: bfloat16 [2, 256, 15360], P('expert'), may hold values from -0.375 to 0.375
- head_weight: bfloat16 [2, 5120, 64], P('expert'), may hold values from -0.078125 to 0.078125
- latent: float32 [2, 2080, 64], P('groups', 'seq'), parts along dimension 0, may hold values from -6 to 6
- timesteps: int32 [2, 2], P('expert', 'groups'), parts along dimension 1, may hold values from 26 to 1000, as said below
- token_order: int32 [2, 2, 2080], P(None, 'groups'), parts along dimension 1, may hold values from 0 to 2079, as said below
Outputs:
- velocity: float32 [2, 2, 2080, 64], P('expert', 'groups', 'seq'), parts along dimension 1
- latents_out: float32 [2, 2, 2080, 64], P('expert', 'groups', 'seq'), parts along dimension 1
There are 2 independent parts, one for each index of `groups`. A program takes and returns all parts, laid end to end along the dimension named above; an argument that names none is the same for every part. Nothing has to cross between parts.
Inputs may be any that keep to these rules, and one draw needn't show every extreme that they name: Each token_order[e, m] is a permutation of 0 to 2079. timesteps[0, m] is at least 876 and timesteps[1, m] at most 875.
All inputs are finite; a program needn't handle non-finite values.
Results may differ from a plain program's by a relative error of at most 0.0085.
Values may be sent and summed in bfloat16 or wider, within the bound.
A program may use at most 192 MiB of HBM per device.

v0:
```python
import jax
import jax.numpy as jnp
from jax import lax
from jax.experimental import pallas as pl
from jax.experimental.pallas import tpu as pltpu
from jax.sharding import PartitionSpec as P


HEAD_DIM = 128
FREQ = 256
HGRID = 20
WGRID = 52
STRIDE = 25


flow_shift = 5.0
norm_eps = 1e-06

DEGREE = 4
CHUNKS = 4
COLUMN_CHUNKS = 2
LOG2E = 1.4426950408889634


def ladder(length):
    return 10000.0 ** (-jnp.arange(length, dtype=jnp.float32) / length)


def rope_angles(tokens):
    half_dim = HEAD_DIM // 2
    side_pairs = half_dim // 3
    frame_pairs = half_dim - 2 * side_pairs
    frame_pos = (tokens // (HGRID * WGRID)).astype(jnp.float32)
    row_pos = (tokens // WGRID % HGRID).astype(jnp.float32)
    column_pos = (tokens % WGRID).astype(jnp.float32)
    return jnp.concatenate(
        [
            frame_pos[:, None] * ladder(frame_pairs),
            row_pos[:, None] * ladder(side_pairs),
            column_pos[:, None] * ladder(side_pairs),
        ],
        axis=1,
    )


def stamp_embedding(step_value):
    half_freq = FREQ // 2
    inverse_rates = 10000.0 ** (-jnp.arange(half_freq, dtype=jnp.float32) / half_freq)
    phases = step_value * inverse_rates
    return jnp.concatenate([jnp.cos(phases), jnp.sin(phases)])


def noise_level(step_value):
    scaled = step_value / 1000.0
    return flow_shift * scaled / (1.0 + (flow_shift - 1.0) * scaled)


def swap(value, axis, flip):
    return lax.ppermute(value, axis, [(i, i ^ flip) for i in range(lax.axis_size(axis))])


def turn_kernel(place_ref, q_ref, k_ref, v_ref, cos_ref, next_ref, prev_ref, out_ref):
    cosine = cos_ref[...]
    from_next = next_ref[...]
    from_prev = prev_ref[...]

    def turned(field):
        ahead = pltpu.roll(field, HEAD_DIM - 1, 1)
        behind = pltpu.roll(field, 1, 1)
        return field * cosine + ahead * from_next + behind * from_prev

    heads = q_ref.shape[1] // HEAD_DIM
    for head in range(heads):
        cols = pl.ds(head * HEAD_DIM, HEAD_DIM)
        turned_k = turned(k_ref[:, cols].astype(jnp.float32))
        turned_q = turned(q_ref[:, cols].astype(jnp.float32)) * (LOG2E * HEAD_DIM**-0.5)
        out_ref[:, pl.ds(2 * head * HEAD_DIM, HEAD_DIM)] = turned_k.astype(jnp.bfloat16)
        out_ref[:, pl.ds((2 * head + 1) * HEAD_DIM, HEAD_DIM)] = v_ref[:, cols]
        out_ref[:, pl.ds((2 * heads + head) * HEAD_DIM, HEAD_DIM)] = turned_q.astype(jnp.bfloat16)


def turn(place, queries, keys, values, tables, flip, chunk, width):
    rows = queries.shape[0]
    pick = lambda i, place_ref: (0, (place_ref[0] ^ flip) * CHUNKS + chunk)
    fixed = lambda i, place_ref: (0, 0)
    return pl.pallas_call(
        turn_kernel,
        grid_spec=pltpu.PrefetchScalarGridSpec(
            num_scalar_prefetch=1,
            grid=(1,),
            in_specs=[pl.BlockSpec((rows, width), pick)] * 3
            + [pl.BlockSpec((rows, HEAD_DIM), fixed)] * 3,
            out_specs=pl.BlockSpec((rows, 3 * width), fixed),
        ),
        out_shape=jax.ShapeDtypeStruct((rows, 3 * width), jnp.bfloat16),
        cost_estimate=pl.CostEstimate(
            flops=20 * rows * width, bytes_accessed=12 * rows * width, transcendentals=0
        ),
        name="turn",
    )(place, queries, keys, values, *tables)


def attend_kernel(near_count, far_count, padded, *refs):
    pairs = refs[: near_count + far_count]
    asking = refs[near_count + far_count : 2 * near_count + far_count]
    out_ref, k_scr, v_scr = refs[2 * near_count + far_count :]
    rows = pairs[0].shape[0]

    @pl.when(pl.program_id(0) == 0)
    def _():
        k_scr[...] = jnp.zeros_like(k_scr)
        v_scr[...] = jnp.zeros_like(v_scr)

    for slot, block in enumerate(pairs):
        k_scr[pl.ds(slot * padded, rows), :] = block[:, :HEAD_DIM]
        v_scr[pl.ds(slot * padded, rows), :] = block[:, HEAD_DIM:]
    spot = lax.broadcasted_iota(jnp.int32, (1, k_scr.shape[0]), 1) % padded
    hide = jnp.where(spot < rows, 0.0, -1e30).astype(jnp.float32)
    for slot, block in enumerate(asking):
        scores = (
            lax.dot_general(
                block[...], k_scr[...], (((1,), (1,)), ((), ())), preferred_element_type=jnp.float32
            )
            + hide
        )
        top = jnp.max(scores, axis=1, keepdims=True)
        weights = jnp.exp2(scores - top)
        total = jnp.sum(weights, axis=1, keepdims=True)
        mixed = jnp.dot(
            weights.astype(jnp.bfloat16), v_scr[...], preferred_element_type=jnp.float32
        )
        out_ref[slot] = (mixed / total).astype(jnp.bfloat16)


def attend(near, far, width):
    rows = near[0].shape[0]
    padded = -(-rows // 16) * 16
    blocks = len(near) + len(far)
    keys = blocks * padded
    heads = width // HEAD_DIM
    work = len(near) * rows * keys * width
    return pl.pallas_call(
        lambda *refs: attend_kernel(len(near), len(far), padded, *refs),
        grid=(heads,),
        in_specs=[pl.BlockSpec((rows, 2 * HEAD_DIM), lambda h: (0, h))] * blocks
        + [pl.BlockSpec((rows, HEAD_DIM), lambda h: (0, 2 * heads + h))] * len(near),
        out_specs=pl.BlockSpec((len(near), rows, HEAD_DIM), lambda h: (0, 0, h)),
        out_shape=jax.ShapeDtypeStruct((len(near), rows, width), jnp.bfloat16),
        scratch_shapes=[pltpu.VMEM((keys, HEAD_DIM), jnp.bfloat16)] * 2,
        cost_estimate=pl.CostEstimate(
            flops=4 * work, bytes_accessed=8 * blocks * rows * width, transcendentals=work // HEAD_DIM
        ),
        name="attend",
    )(*near, *far, *near)


def project_kernel(count, *refs):
    weight_ref, out_ref = refs[count:]
    total, start = 0.0, 0
    for left in refs[:count]:
        depth = left.shape[1]
        total += jnp.dot(
            left[...], weight_ref[pl.ds(start, depth), :], preferred_element_type=jnp.float32
        )
        start += depth
    out_ref[...] = total.astype(out_ref.dtype)


def project(slot, chunk, lefts, weight, dtype):
    rows = lefts[0].shape[1]
    depth = weight.shape[0]
    columns = weight.shape[1] // COLUMN_CHUNKS
    tiles = 10
    tile = columns // tiles
    return pl.pallas_call(
        lambda *refs: project_kernel(len(lefts), *refs),
        grid=(tiles,),
        in_specs=[pl.BlockSpec((None, rows, left.shape[2]), lambda t: (slot, 0, 0)) for left in lefts]
        + [pl.BlockSpec((depth, tile), lambda t: (0, chunk * tiles + t))],
        out_specs=pl.BlockSpec((rows, tile), lambda t: (0, t)),
        out_shape=jax.ShapeDtypeStruct((rows, columns), dtype),
        cost_estimate=pl.CostEstimate(
            flops=2 * rows * depth * columns,
            bytes_accessed=2 * depth * (columns + rows) + 4 * rows * columns,
            transcendentals=0,
        ),
        name="project",
    )(*lefts, weight)


def shards(
    query_heads,
    key_heads,
    value_heads,
    residual,
    out_weight,
    mod_weight,
    head_weight,
    latent,
    timesteps,
    token_order,
):
    seq_count = lax.axis_size("seq")
    seq_index = lax.axis_index("seq")
    expert_index = lax.axis_index("expert")
    group_count = lax.axis_size("groups")
    group_bit = lax.axis_index("groups") & 1
    cycle_count = seq_count // DEGREE
    place = seq_index // cycle_count
    cycle = seq_index % cycle_count
    rows = query_heads.shape[2]
    model_width = residual.shape[3]
    stored = out_weight.shape[1]
    width = cycle_count * stored // CHUNKS

    own_weight = out_weight[0]
    weight = jnp.zeros((cycle_count * stored, model_width), own_weight.dtype)
    weight = lax.dynamic_update_slice_in_dim(weight, own_weight, cycle * stored, 0)
    for flip in range(1, cycle_count):
        base = (cycle ^ flip) * stored
        if group_count % 2 == 0:
            half = stored // 2
            mine = lax.dynamic_slice_in_dim(own_weight, group_bit * half, half, 0)
            first = swap(mine, "seq", flip)
            second = swap(first, "groups", 1)
            weight = lax.dynamic_update_slice_in_dim(weight, first, base + group_bit * half, 0)
            weight = lax.dynamic_update_slice_in_dim(weight, second, base + (1 - group_bit) * half, 0)
        else:
            weight = lax.dynamic_update_slice_in_dim(weight, swap(own_weight, "seq", flip), base, 0)

    orders = lax.dynamic_index_in_dim(token_order, expert_index, 0, keepdims=False)[0]
    own_tokens = lax.dynamic_slice_in_dim(orders, seq_index * rows, rows)
    angles = jnp.repeat(rope_angles(own_tokens), 2, axis=1)
    odd = (jnp.arange(HEAD_DIM) % 2 == 1)[None]
    sine = jnp.sin(angles)
    tables = (jnp.cos(angles), jnp.where(odd, 0.0, -sine), jnp.where(odd, sine, 0.0))
    place_arr = place[None].astype(jnp.int32)

    mixed = []
    for chunk in range(CHUNKS):
        near, far = [], []
        for flip in (3, 2, 1, 0):
            block = turn(
                place_arr,
                query_heads[0, 0],
                key_heads[0, 0],
                value_heads[0, 0],
                tables,
                flip,
                chunk,
                width,
            )
            if flip:
                block = swap(block, "seq", flip * cycle_count)
            near.append(block)
        near = near[::-1]
        for block in near:
            for flip in range(1, cycle_count):
                far.append(swap(block[:, : 2 * width], "seq", flip))
        mixed.append(attend(near, far, width))

    step_value = timesteps[0, 0].astype(jnp.float32)
    embedded = stamp_embedding(step_value).astype(jnp.bfloat16)
    modulation = jnp.dot(embedded[None], mod_weight[0], preferred_element_type=jnp.float32)[0]
    gate_vec = modulation[:model_width]
    shift_vec = modulation[model_width : 2 * model_width]
    scale_vec = modulation[2 * model_width :]

    columns = model_width // COLUMN_CHUNKS
    hidden = []
    for chunk in range(COLUMN_CHUNKS):
        span = slice(chunk * columns, (chunk + 1) * columns)
        far_sum = swap(project(3, chunk, mixed, weight, jnp.bfloat16), "seq", cycle_count)
        near_sum = swap(project(1, chunk, mixed, weight, jnp.bfloat16), "seq", cycle_count)
        passed = project(2, chunk, mixed, weight, jnp.float32) + far_sum.astype(jnp.float32)
        passed = swap(passed.astype(jnp.bfloat16), "seq", 2 * cycle_count)
        kept = project(0, chunk, mixed, weight, jnp.float32) + near_sum.astype(jnp.float32)
        projected = kept + passed.astype(jnp.float32)
        hidden.append(residual[0, 0, :, span].astype(jnp.float32) + gate_vec[span] * projected)
    mean = sum(jnp.sum(part, axis=1, keepdims=True) for part in hidden) / model_width
    centered = [part - mean for part in hidden]
    variance = sum(jnp.sum(part * part, axis=1, keepdims=True) for part in centered) / model_width
    inverse_std = lax.rsqrt(variance + norm_eps)
    velocity = 0.0
    for chunk in range(COLUMN_CHUNKS):
        span = slice(chunk * columns, (chunk + 1) * columns)
        normed = (centered[chunk] * inverse_std * (1.0 + scale_vec[span]) + shift_vec[span]).astype(
            jnp.bfloat16
        )
        velocity += jnp.dot(normed, head_weight[0, span], preferred_element_type=jnp.float32)
    change = noise_level(step_value - STRIDE) - noise_level(step_value)
    stepped = latent[0] + change * velocity
    arrived = lax.ppermute(stepped.astype(jnp.bfloat16), "expert", [(0, 1)])[None]
    positions = seq_index[None]
    flip = seq_count // 2
    while flip:
        route = [(seq_count + i, seq_count + (i ^ flip)) for i in range(seq_count)]
        arrived = jnp.concatenate([arrived, lax.ppermute(arrived, ("expert", "seq"), route)], axis=0)
        positions = jnp.concatenate([positions, positions ^ flip])
        flip //= 2
    first_order = token_order[0, 0].reshape(seq_count, rows)[positions].reshape(-1)
    chosen = (own_tokens[:, None] == first_order[None]).astype(jnp.bfloat16)
    started = jnp.dot(
        chosen, arrived.reshape(seq_count * rows, -1), preferred_element_type=jnp.float32
    )
    finished = jnp.where(expert_index == 0, stepped, started + change * velocity)
    return (velocity[None, None], finished[None, None])


def solution(mesh):
    return jax.shard_map(
        shards,
        mesh=mesh,
        in_specs=(
            P("expert", "groups", "seq", None),
            P("expert", "groups", "seq", None),
            P("expert", "groups", "seq", None),
            P("expert", "groups", "seq", None),
            P("expert", "seq", None),
            P("expert", None, None),
            P("expert", None, None),
            P("groups", "seq", None),
            P("expert", "groups"),
            P(None, "groups", None),
        ),
        out_specs=(P("expert", "groups", "seq", None), P("expert", "groups", "seq", None)),
        check_vma=False,
    )
```

profile of v0, /device:TPU:1, one launch (start us, length us, event | category | flops | bytes accessed | tf_op | source)
XLA Modules:
  0.0 525.4 jit_solution(3173683864144155629)
XLA Ops:
  31.9 36.9 %collective-permute-done.3.refs_4_ = bf16[260,512]{1,0:T(8,128)(2,1)} collective-permute-done((bf16[260,512]{1,0:T(8,128)(2,1)}, bf16[260,512]{1,0:T(8,128)(2,1)}, u32[]{:S(2)}, u32[]{:S(2)}) %collective-permute-start.3) | collective-permute-done | bytes 266272 | tf_op jit(solution)/shard_map/ppermute | solution.py:59
  92.9 5.9 %collective-permute-done.1.refs_2_.refs_10_ = bf16[260,768]{1,0:T(8,128)(2,1)} collective-permute-done((bf16[260,768]{1,0:T(8,128)(2,1)}, bf16[260,768]{1,0:T(8,128)(2,1)}, u32[]{:S(2)}, u32[]{:S(2)}) %collective-permute-start.1) | collective-permute-done | bytes 399392 | tf_op jit(solution)/shard_map/ppermute | solution.py:59
  98.8 5.1 collective-permute-start.9
  103.9 21.2 %collective-permute-start.14 = (bf16[260,768]{1,0:T(8,128)(2,1)S(1)}, bf16[260,768]{1,0:T(8,128)(2,1)}, u32[]{:S(2)}, u32[]{:S(2)}) collective-permute-start(bf16[260,768]{1,0:T(8,128)(2,1)S(1)} %copy-done.5), channel_id=1, source_target_pairs={{0,2},{1,3},{2,0},{3,1},{4,6},{5,7},{6,4},{7,5},{8,10},{9,11},{10,... | collective-permute-start | bytes 1198088 | tf_op jit(solution)/shard_map/ppermute | solution.py:59
  132.6 4.5 collective-permute-start.16
  143.8 16.1 %collective-permute-start.21 = (bf16[260,768]{1,0:T(8,128)(2,1)}, bf16[260,768]{1,0:T(8,128)(2,1)S(1)}, u32[]{:S(2)}, u32[]{:S(2)}) collective-permute-start(bf16[260,768]{1,0:T(8,128)(2,1)} %turn.29), channel_id=1, source_target_pairs={{0,2},{1,3},{2,0},{3,1},{4,6},{5,7},{6,4},{7,5},{8,10},{9,11},{10,... | collective-permute-start | bytes 1198088 | tf_op jit(solution)/shard_map/ppermute | solution.py:59
  161.9 5.4 %collective-permute-done.15.refs_2_.refs_10_ = bf16[260,768]{1,0:T(8,128)(2,1)} collective-permute-done((bf16[260,768]{1,0:T(8,128)(2,1)}, bf16[260,768]{1,0:T(8,128)(2,1)}, u32[]{:S(2)}, u32[]{:S(2)}) %collective-permute-start.15) | collective-permute-done | bytes 399392 | tf_op jit(solution)/shard_map/ppermute | solution.py:59
  167.4 4.1 collective-permute-start.23
  180.8 21.3 %collective-permute-done.22.refs_2_.refs_10_ = bf16[260,768]{1,0:T(8,128)(2,1)S(1)} collective-permute-done((bf16[260,768]{1,0:T(8,128)(2,1)S(1)}, bf16[260,768]{1,0:T(8,128)(2,1)S(1)}, u32[]{:S(2)}, u32[]{:S(2)}) %collective-permute-start.22) | collective-permute-done | bytes 399392 | tf_op jit(solution)/shard_map/ppermute | solution.py:59
  214.7 4.8 collective-permute-done.12.refs_6_
  221.7 5.3 %broadcast_in_dim.70 = bf16[1024,5120]{1,0:T(8,128)(2,1)} broadcast(bf16[]{:T(256)} %constant.146.clone.1), dimensions={} | broadcast | bytes 10485762 | tf_op jit(solution)/shard_map/broadcast_in_dim | solution.py:217
  238.7 10.7 %attend.4.refs_0_ = bf16[4,260,256]{2,1,0:T(8,128)(2,1)} custom-call(bf16[260,768]{1,0:T(8,128)(2,1)} %turn.16.refs_0_.refs_8_, bf16[260,768]{1,0:T(8,128)(2,1)} %collective-permute-done.refs_1_.refs_9_, bf16[260,768]{1,0:T(8,128)(2,1)} %collective-permute-done.1.refs_2_.refs_10_, bf16[260,768]{1,0:T(8,128)(2,1)} %collective-permute-done.2.refs_3_.refs_11_, ...), custom_call_target="tpu_custom_call" | custom-call | flops 2317352960 | bytes 4259840 | tf_op jit(solution)/shard_map/attend/pallas_call | solution.py:142
  252.4 10.6 %attend.5.refs_1_ = bf16[4,260,256]{2,1,0:T(8,128)(2,1)} custom-call(bf16[260,768]{1,0:T(8,128)(2,1)} %turn.20.refs_0_.refs_8_, bf16[260,768]{1,0:T(8,128)(2,1)} %collective-permute-done.7.refs_1_.refs_9_, bf16[260,768]{1,0:T(8,128)(2,1)} %collective-permute-done.8.refs_2_.refs_10_, bf16[260,768]{1,0:T(8,128)(2,1)} %collective-permute-done.9.refs_3_.refs_11_, ...), custom_call_target="tpu_custom_call" | custom-call | flops 2317352960 | bytes 4259840 | tf_op jit(solution)/shard_map/attend/pallas_call | solution.py:142
  263.0 10.8 %attend.6.refs_2_ = bf16[4,260,256]{2,1,0:T(8,128)(2,1)} custom-call(bf16[260,768]{1,0:T(8,128)(2,1)} %turn.24.refs_0_.refs_8_, bf16[260,768]{1,0:T(8,128)(2,1)} %collective-permute-done.14.refs_1_.refs_9_, bf16[260,768]{1,0:T(8,128)(2,1)} %collective-permute-done.15.refs_2_.refs_10_, bf16[260,768]{1,0:T(8,128)(2,1)} %collective-permute-done.16.refs_3_.refs_11_, ...), custom_call_target="tpu_custom_call" | custom-call | flops 2317352960 | bytes 4259840 | tf_op jit(solution)/shard_map/attend/pallas_call | solution.py:142
  275.3 10.6 %attend.7.refs_3_ = bf16[4,260,256]{2,1,0:T(8,128)(2,1)} custom-call(bf16[260,768]{1,0:T(8,128)(2,1)} %turn.28.refs_0_.refs_8_, bf16[260,768]{1,0:T(8,128)(2,1)} %copy-done.6, bf16[260,768]{1,0:T(8,128)(2,1)} %copy-done.7, bf16[260,768]{1,0:T(8,128)(2,1)} %copy-done.8, bf16[260,512]{1,0:T(8,128)(2,1)} %collective-permute-done.24.refs_4_, ...), custom_call_target="tpu_custom_call" | custom-call | flops 2317352960 | bytes 4259840 | tf_op jit(solution)/shard_map/attend/pallas_call | solution.py:142
  291.0 8.6 %project.11 = bf16[260,2560]{1,0:T(8,128)(2,1)} custom-call(bf16[4,260,256]{2,1,0:T(8,128)(2,1)} %attend.4.refs_0_, bf16[4,260,256]{2,1,0:T(8,128)(2,1)} %attend.5.refs_1_, bf16[4,260,256]{2,1,0:T(8,128)(2,1)} %attend.6.refs_2_, bf16[4,260,256]{2,1,0:T(8,128)(2,1)} %attend.7.refs_3_, bf16[1024,5120]{1,0:T(8,128)(2,1)} %constant_dynamic-update-slice_fusion.refs_4_), custom_call_target="tpu_custom_call" | custom-call | flops 1363148800 | bytes 8437760 | tf_op jit(solution)/shard_map/project/pallas_call | solution.py:175
  299.6 7.5 %collective-permute-start.31 = (bf16[260,2560]{1,0:T(8,128)(2,1)}, bf16[260,2560]{1,0:T(8,128)(2,1)}, u32[]{:S(2)}, u32[]{:S(2)}) collective-permute-start(bf16[260,2560]{1,0:T(8,128)(2,1)} %project.11), channel_id=1, source_target_pairs={{0,2},{1,3},{2,0},{3,1},{4,6},{5,7},{6,4},{7,5},{8,10},{9,11},{10,... | collective-permute-start | bytes 3993608 | tf_op jit(solution)/shard_map/ppermute | solution.py:59
  307.1 8.6 %project.15 = bf16[260,2560]{1,0:T(8,128)(2,1)} custom-call(bf16[4,260,256]{2,1,0:T(8,128)(2,1)} %attend.4.refs_0_, bf16[4,260,256]{2,1,0:T(8,128)(2,1)} %attend.5.refs_1_, bf16[4,260,256]{2,1,0:T(8,128)(2,1)} %attend.6.refs_2_, bf16[4,260,256]{2,1,0:T(8,128)(2,1)} %attend.7.refs_3_, bf16[1024,5120]{1,0:T(8,128)(2,1)} %constant_dynamic-update-slice_fusion.refs_4_), custom_call_target="tpu_custom_call" | custom-call | flops 1363148800 | bytes 8437760 | tf_op jit(solution)/shard_map/project/pallas_call | solution.py:175
  315.8 8.6 %project.9 = bf16[260,2560]{1,0:T(8,128)(2,1)} custom-call(bf16[4,260,256]{2,1,0:T(8,128)(2,1)} %attend.4.refs_0_, bf16[4,260,256]{2,1,0:T(8,128)(2,1)} %attend.5.refs_1_, bf16[4,260,256]{2,1,0:T(8,128)(2,1)} %attend.6.refs_2_, bf16[4,260,256]{2,1,0:T(8,128)(2,1)} %attend.7.refs_3_, bf16[1024,5120]{1,0:T(8,128)(2,1)} %constant_dynamic-update-slice_fusion.refs_4_), custom_call_target="tpu_custom_call" | custom-call | flops 1363148800 | bytes 8437760 | tf_op jit(solution)/shard_map/project/pallas_call | solution.py:175
  325.9 8.6 %project.13 = bf16[260,2560]{1,0:T(8,128)(2,1)} custom-call(bf16[4,260,256]{2,1,0:T(8,128)(2,1)} %attend.4.refs_0_, bf16[4,260,256]{2,1,0:T(8,128)(2,1)} %attend.5.refs_1_, bf16[4,260,256]{2,1,0:T(8,128)(2,1)} %attend.6.refs_2_, bf16[4,260,256]{2,1,0:T(8,128)(2,1)} %attend.7.refs_3_, bf16[1024,5120]{1,0:T(8,128)(2,1)} %constant_dynamic-update-slice_fusion.refs_4_), custom_call_target="tpu_custom_call" | custom-call | flops 1363148800 | bytes 8437760 | tf_op jit(solution)/shard_map/project/pallas_call | solution.py:175
  334.5 8.9 %project.10 = f32[260,2560]{1,0:T(8,128)} custom-call(bf16[4,260,256]{2,1,0:T(8,128)(2,1)} %attend.4.refs_0_, bf16[4,260,256]{2,1,0:T(8,128)(2,1)} %attend.5.refs_1_, bf16[4,260,256]{2,1,0:T(8,128)(2,1)} %attend.6.refs_2_, bf16[4,260,256]{2,1,0:T(8,128)(2,1)} %attend.7.refs_3_, bf16[1024,5120]{1,0:T(8,128)(2,1)} %constant_dynamic-update-slice_fusion.refs_4_), custom_call_target="tpu_custom_call" | custom-call | flops 1363148800 | bytes 8437760 | tf_op jit(solution)/shard_map/project/pallas_call | solution.py:175
  343.4 9.1 %project.14 = f32[260,2560]{1,0:T(8,128)} custom-call(bf16[4,260,256]{2,1,0:T(8,128)(2,1)} %attend.4.refs_0_, bf16[4,260,256]{2,1,0:T(8,128)(2,1)} %attend.5.refs_1_, bf16[4,260,256]{2,1,0:T(8,128)(2,1)} %attend.6.refs_2_, bf16[4,260,256]{2,1,0:T(8,128)(2,1)} %attend.7.refs_3_, bf16[1024,5120]{1,0:T(8,128)(2,1)} %constant_dynamic-update-slice_fusion.refs_4_), custom_call_target="tpu_custom_call" | custom-call | flops 1363148800 | bytes 8437760 | tf_op jit(solution)/shard_map/project/pallas_call | solution.py:175
  358.7 31.6 %collective-permute-done.34 = bf16[260,2560]{1,0:T(8,128)(2,1)} collective-permute-done((bf16[260,2560]{1,0:T(8,128)(2,1)}, bf16[260,2560]{1,0:T(8,128)(2,1)}, u32[]{:S(2)}, u32[]{:S(2)}) %collective-permute-start.34) | collective-permute-done | bytes 1331232 | tf_op jit(solution)/shard_map/ppermute | solution.py:59
  395.8 4.4 fusion
  400.2 8.9 %project.8 = f32[260,2560]{1,0:T(8,128)} custom-call(bf16[4,260,256]{2,1,0:T(8,128)(2,1)} %attend.4.refs_0_, bf16[4,260,256]{2,1,0:T(8,128)(2,1)} %attend.5.refs_1_, bf16[4,260,256]{2,1,0:T(8,128)(2,1)} %attend.6.refs_2_, bf16[4,260,256]{2,1,0:T(8,128)(2,1)} %attend.7.refs_3_, bf16[1024,5120]{1,0:T(8,128)(2,1)} %constant_dynamic-update-slice_fusion.refs_4_), custom_call_target="tpu_custom_call" | custom-call | flops 1363148800 | bytes 8437760 | tf_op jit(solution)/shard_map/project/pallas_call | solution.py:175
  409.1 9.1 %project.12 = f32[260,2560]{1,0:T(8,128)} custom-call(bf16[4,260,256]{2,1,0:T(8,128)(2,1)} %attend.4.refs_0_, bf16[4,260,256]{2,1,0:T(8,128)(2,1)} %attend.5.refs_1_, bf16[4,260,256]{2,1,0:T(8,128)(2,1)} %attend.6.refs_2_, bf16[4,260,256]{2,1,0:T(8,128)(2,1)} %attend.7.refs_3_, bf16[1024,5120]{1,0:T(8,128)(2,1)} %constant_dynamic-update-slice_fusion.refs_4_), custom_call_target="tpu_custom_call" | custom-call | flops 1363148800 | bytes 8437760 | tf_op jit(solution)/shard_map/project/pallas_call | solution.py:175
  418.2 20.5 %collective-permute-done.30 = bf16[260,2560]{1,0:T(8,128)(2,1)} collective-permute-done((bf16[260,2560]{1,0:T(8,128)(2,1)}, bf16[260,2560]{1,0:T(8,128)(2,1)}, u32[]{:S(2)}, u32[]{:S(2)}) %collective-permute-start.30) | collective-permute-done | bytes 1331232 | tf_op jit(solution)/shard_map/ppermute | solution.py:59
  438.7 29.0 %collective-permute-done.33 = bf16[260,2560]{1,0:T(8,128)(2,1)} collective-permute-done((bf16[260,2560]{1,0:T(8,128)(2,1)}, bf16[260,2560]{1,0:T(8,128)(2,1)}, u32[]{:S(2)}, u32[]{:S(2)}) %collective-permute-start.33) | collective-permute-done | bytes 1331232 | tf_op jit(solution)/shard_map/ppermute | solution.py:59
  467.7 8.6 %collective-permute-done.35 = bf16[260,2560]{1,0:T(8,128)(2,1)} collective-permute-done((bf16[260,2560]{1,0:T(8,128)(2,1)}, bf16[260,2560]{1,0:T(8,128)(2,1)}, u32[]{:S(2)}, u32[]{:S(2)}) %collective-permute-start.35) | collective-permute-done | bytes 1331232 | tf_op jit(solution)/shard_map/ppermute | solution.py:59
  476.3 5.6 %fusion.34 = (f32[260]{0:T(512)S(1)}, f32[260,2560]{1,0:T(8,128)S(1)}, f32[260]{0:T(512)S(1)}, f32[260,2560]{1,0:T(8,128)S(1)}) fusion(bf16[260,2560]{1,0:T(8,128)(2,1)} %collective-permute-done.32, f32[260,2560]{1,0:T(8,128)S(1)} %copy-done.2, bf16[260,2560]{1,0:T(8,128)(2,1)} %collective-permute-done.30, f32[2560]{0:T(1024)S(1)} %get-tuple-element.19, ...), kind=kLoop, calls=%fused_computation.75 | loop fusion | flops 10649080 | bytes 18659360 | tf_op jit(solution)/shard_map/reduce_sum | solution.py:280
  485.9 20.0 %collective-permute-done.36 = bf16[260,64]{0,1:T(8,128)(2,1)S(1)} collective-permute-done((bf16[260,64]{0,1:T(8,128)(2,1)S(1)}, bf16[260,64]{0,1:T(8,128)(2,1)S(1)}, u32[]{:S(2)}, u32[]{:S(2)}) %collective-permute-start.36) | collective-permute-done | bytes 33312 | tf_op jit(solution)/shard_map/ppermute | solution.py:293
  507.9 3.7 collective-permute-done.37
  (179 shorter events, 149.0 us)
Async XLA Ops:
  4.1 216.4 %collective-permute-start.28 = (bf16[256,5120]{1,0:T(8,128)(2,1)}, bf16[256,5120]{1,0:T(8,128)(2,1)S(1)}, u32[]{:S(2)}, u32[]{:S(2)}) collective-permute-start(bf16[256,5120]{1,0:T(8,128)(2,1)} %dynamic-slice_bitcast_fusion), channel_id=1, source_target_pairs={{0,1},{1,0},{2,3},{3,2},{4,5},{5,4},{6,7},{7,6},{8,9},{9,8},{10,11... | collective-permute-start | bytes 7864328 | tf_op jit(solution)/shard_map/ppermute | solution.py:59
  12.8 56.0 %collective-permute-start.3 = (bf16[260,512]{1,0:T(8,128)(2,1)}, bf16[260,512]{1,0:T(8,128)(2,1)}, u32[]{:S(2)}, u32[]{:S(2)}) collective-permute-start(bf16[260,512]{1,0:T(8,128)(2,1)} %slice.122), channel_id=1, source_target_pairs={{0,1},{1,0},{2,3},{3,2},{4,5},{5,4},{6,7},{7,6},{8,9},{9,8},{10,11... | collective-permute-start | bytes 798728 | tf_op jit(solution)/shard_map/ppermute | solution.py:59
  16.7 57.9 %collective-permute-start.10 = (bf16[260,512]{1,0:T(8,128)(2,1)}, bf16[260,512]{1,0:T(8,128)(2,1)}, u32[]{:S(2)}, u32[]{:S(2)}) collective-permute-start(bf16[260,512]{1,0:T(8,128)(2,1)} %slice.126), channel_id=1, source_target_pairs={{0,1},{1,0},{2,3},{3,2},{4,5},{5,4},{6,7},{7,6},{8,9},{9,8},{10,11... | collective-permute-start | bytes 798728 | tf_op jit(solution)/shard_map/ppermute | solution.py:59
  21.3 59.0 %collective-permute-start.17 = (bf16[260,512]{1,0:T(8,128)(2,1)S(1)}, bf16[260,512]{1,0:T(8,128)(2,1)}, u32[]{:S(2)}, u32[]{:S(2)}) collective-permute-start(bf16[260,512]{1,0:T(8,128)(2,1)S(1)} %slice.130), channel_id=1, source_target_pairs={{0,1},{1,0},{2,3},{3,2},{4,5},{5,4},{6,7},{7,6},{8,9},{9,8},{10,11... | collective-permute-start | bytes 798728 | tf_op jit(solution)/shard_map/ppermute | solution.py:59
  23.7 60.2 %collective-permute-start = (bf16[260,768]{1,0:T(8,128)(2,1)}, bf16[260,768]{1,0:T(8,128)(2,1)}, u32[]{:S(2)}, u32[]{:S(2)}) collective-permute-start(bf16[260,768]{1,0:T(8,128)(2,1)} %turn.17), channel_id=1, source_target_pairs={{0,2},{1,3},{2,0},{3,1},{4,6},{5,7},{6,4},{7,5},{8,10},{9,11},{10,... | collective-permute-start | bytes 1198088 | tf_op jit(solution)/shard_map/ppermute | solution.py:59
  68.8 30.0 %collective-permute-start.1 = (bf16[260,768]{1,0:T(8,128)(2,1)}, bf16[260,768]{1,0:T(8,128)(2,1)}, u32[]{:S(2)}, u32[]{:S(2)}) collective-permute-start(bf16[260,768]{1,0:T(8,128)(2,1)} %turn.18), channel_id=1, source_target_pairs={{0,4},{1,5},{2,6},{3,7},{4,0},{5,1},{6,2},{7,3},{8,12},{9,13},{10,... | collective-permute-start | bytes 1198088 | tf_op jit(solution)/shard_map/ppermute | solution.py:59
  74.6 29.3 %collective-permute-start.2 = (bf16[260,768]{1,0:T(8,128)(2,1)S(1)}, bf16[260,768]{1,0:T(8,128)(2,1)}, u32[]{:S(2)}, u32[]{:S(2)}) collective-permute-start(bf16[260,768]{1,0:T(8,128)(2,1)S(1)} %copy-done.4), channel_id=1, source_target_pairs={{0,6},{1,7},{2,4},{3,5},{4,2},{5,3},{6,0},{7,1},{8,14},{9,15},{10,... | collective-permute-start | bytes 1198088 | tf_op jit(solution)/shard_map/ppermute | solution.py:59
  80.4 44.7 %collective-permute-start.7 = (bf16[260,768]{1,0:T(8,128)(2,1)}, bf16[260,768]{1,0:T(8,128)(2,1)}, u32[]{:S(2)}, u32[]{:S(2)}) collective-permute-start(bf16[260,768]{1,0:T(8,128)(2,1)} %turn.21), channel_id=1, source_target_pairs={{0,2},{1,3},{2,0},{3,1},{4,6},{5,7},{6,4},{7,5},{8,10},{9,11},{10,... | collective-permute-start | bytes 1198088 | tf_op jit(solution)/shard_map/ppermute | solution.py:59
  83.9 48.7 %collective-permute-start.8 = (bf16[260,768]{1,0:T(8,128)(2,1)}, bf16[260,768]{1,0:T(8,128)(2,1)}, u32[]{:S(2)}, u32[]{:S(2)}) collective-permute-start(bf16[260,768]{1,0:T(8,128)(2,1)} %turn.22), channel_id=1, source_target_pairs={{0,4},{1,5},{2,6},{3,7},{4,0},{5,1},{6,2},{7,3},{8,12},{9,13},{10,... | collective-permute-start | bytes 1198088 | tf_op jit(solution)/shard_map/ppermute | solution.py:59
  98.8 45.0 %collective-permute-start.9 = (bf16[260,768]{1,0:T(8,128)(2,1)}, bf16[260,768]{1,0:T(8,128)(2,1)}, u32[]{:S(2)}, u32[]{:S(2)}) collective-permute-start(bf16[260,768]{1,0:T(8,128)(2,1)} %turn.23), channel_id=1, source_target_pairs={{0,6},{1,7},{2,4},{3,5},{4,2},{5,3},{6,0},{7,1},{8,14},{9,15},{10,... | collective-permute-start | bytes 1198088 | tf_op jit(solution)/shard_map/ppermute | solution.py:59
  103.9 56.1 %collective-permute-start.14 = (bf16[260,768]{1,0:T(8,128)(2,1)S(1)}, bf16[260,768]{1,0:T(8,128)(2,1)}, u32[]{:S(2)}, u32[]{:S(2)}) collective-permute-start(bf16[260,768]{1,0:T(8,128)(2,1)S(1)} %copy-done.5), channel_id=1, source_target_pairs={{0,2},{1,3},{2,0},{3,1},{4,6},{5,7},{6,4},{7,5},{8,10},{9,11},{10,... | collective-permute-start | bytes 1198088 | tf_op jit(solution)/shard_map/ppermute | solution.py:59
  125.0 42.3 %collective-permute-start.15 = (bf16[260,768]{1,0:T(8,128)(2,1)}, bf16[260,768]{1,0:T(8,128)(2,1)}, u32[]{:S(2)}, u32[]{:S(2)}) collective-permute-start(bf16[260,768]{1,0:T(8,128)(2,1)} %turn.26), channel_id=1, source_target_pairs={{0,4},{1,5},{2,6},{3,7},{4,0},{5,1},{6,2},{7,3},{8,12},{9,13},{10,... | collective-permute-start | bytes 1198088 | tf_op jit(solution)/shard_map/ppermute | solution.py:59
  132.6 39.9 %collective-permute-start.16 = (bf16[260,768]{1,0:T(8,128)(2,1)}, bf16[260,768]{1,0:T(8,128)(2,1)}, u32[]{:S(2)}, u32[]{:S(2)}) collective-permute-start(bf16[260,768]{1,0:T(8,128)(2,1)} %turn.27), channel_id=1, source_target_pairs={{0,6},{1,7},{2,4},{3,5},{4,2},{5,3},{6,0},{7,1},{8,14},{9,15},{10,... | collective-permute-start | bytes 1198088 | tf_op jit(solution)/shard_map/ppermute | solution.py:59
  143.8 36.7 %collective-permute-start.21 = (bf16[260,768]{1,0:T(8,128)(2,1)}, bf16[260,768]{1,0:T(8,128)(2,1)S(1)}, u32[]{:S(2)}, u32[]{:S(2)}) collective-permute-start(bf16[260,768]{1,0:T(8,128)(2,1)} %turn.29), channel_id=1, source_target_pairs={{0,2},{1,3},{2,0},{3,1},{4,6},{5,7},{6,4},{7,5},{8,10},{9,11},{10,... | collective-permute-start | bytes 1198088 | tf_op jit(solution)/shard_map/ppermute | solution.py:59
  159.9 42.1 %collective-permute-start.22 = (bf16[260,768]{1,0:T(8,128)(2,1)S(1)}, bf16[260,768]{1,0:T(8,128)(2,1)S(1)}, u32[]{:S(2)}, u32[]{:S(2)}) collective-permute-start(bf16[260,768]{1,0:T(8,128)(2,1)S(1)} %copy-done.3), channel_id=1, source_target_pairs={{0,4},{1,5},{2,6},{3,7},{4,0},{5,1},{6,2},{7,3},{8,12},{9,13},{10,... | collective-permute-start | bytes 1198088 | tf_op jit(solution)/shard_map/ppermute | solution.py:59
  167.4 35.8 %collective-permute-start.23 = (bf16[260,768]{1,0:T(8,128)(2,1)}, bf16[260,768]{1,0:T(8,128)(2,1)S(1)}, u32[]{:S(2)}, u32[]{:S(2)}) collective-permute-start(bf16[260,768]{1,0:T(8,128)(2,1)} %turn.31), channel_id=1, source_target_pairs={{0,6},{1,7},{2,4},{3,5},{4,2},{5,3},{6,0},{7,1},{8,14},{9,15},{10,... | collective-permute-start | bytes 1198088 | tf_op jit(solution)/shard_map/ppermute | solution.py:59
  172.5 31.0 %collective-permute-start.4 = (bf16[260,512]{1,0:T(8,128)(2,1)S(1)}, bf16[260,512]{1,0:T(8,128)(2,1)S(1)}, u32[]{:S(2)}, u32[]{:S(2)}) collective-permute-start(bf16[260,512]{1,0:T(8,128)(2,1)S(1)} %slice.123), channel_id=1, source_target_pairs={{0,1},{1,0},{2,3},{3,2},{4,5},{5,4},{6,7},{7,6},{8,9},{9,8},{10,11... | collective-permute-start | bytes 798728 | tf_op jit(solution)/shard_map/ppermute | solution.py:59
  180.5 29.0 %collective-permute-start.5 = (bf16[260,512]{1,0:T(8,128)(2,1)}, bf16[260,512]{1,0:T(8,128)(2,1)}, u32[]{:S(2)}, u32[]{:S(2)}) collective-permute-start(bf16[260,512]{1,0:T(8,128)(2,1)} %slice.124), channel_id=1, source_target_pairs={{0,1},{1,0},{2,3},{3,2},{4,5},{5,4},{6,7},{7,6},{8,9},{9,8},{10,11... | collective-permute-start | bytes 798728 | tf_op jit(solution)/shard_map/ppermute | solution.py:59
  209.6 39.9 %collective-permute-start.13 = (bf16[260,512]{1,0:T(8,128)(2,1)}, bf16[260,512]{1,0:T(8,128)(2,1)}, u32[]{:S(2)}, u32[]{:S(2)}) collective-permute-start(bf16[260,512]{1,0:T(8,128)(2,1)} %slice.129), channel_id=1, source_target_pairs={{0,1},{1,0},{2,3},{3,2},{4,5},{5,4},{6,7},{7,6},{8,9},{9,8},{10,11... | collective-permute-start | bytes 798728 | tf_op jit(solution)/shard_map/ppermute | solution.py:59
  210.3 39.5 %collective-permute-start.18 = (bf16[260,512]{1,0:T(8,128)(2,1)S(1)}, bf16[260,512]{1,0:T(8,128)(2,1)}, u32[]{:S(2)}, u32[]{:S(2)}) collective-permute-start(bf16[260,512]{1,0:T(8,128)(2,1)S(1)} %slice.131), channel_id=1, source_target_pairs={{0,1},{1,0},{2,3},{3,2},{4,5},{5,4},{6,7},{7,6},{8,9},{9,8},{10,11... | collective-permute-start | bytes 798728 | tf_op jit(solution)/shard_map/ppermute | solution.py:59
  213.7 37.3 %collective-permute-start.19 = (bf16[260,512]{1,0:T(8,128)(2,1)S(1)}, bf16[260,512]{1,0:T(8,128)(2,1)}, u32[]{:S(2)}, u32[]{:S(2)}) collective-permute-start(bf16[260,512]{1,0:T(8,128)(2,1)S(1)} %slice.132), channel_id=1, source_target_pairs={{0,1},{1,0},{2,3},{3,2},{4,5},{5,4},{6,7},{7,6},{8,9},{9,8},{10,11... | collective-permute-start | bytes 798728 | tf_op jit(solution)/shard_map/ppermute | solution.py:59
  219.5 31.8 %collective-permute-start.20 = (bf16[260,512]{1,0:T(8,128)(2,1)S(1)}, bf16[260,512]{1,0:T(8,128)(2,1)}, u32[]{:S(2)}, u32[]{:S(2)}) collective-permute-start(bf16[260,512]{1,0:T(8,128)(2,1)S(1)} %slice.133), channel_id=1, source_target_pairs={{0,1},{1,0},{2,3},{3,2},{4,5},{5,4},{6,7},{7,6},{8,9},{9,8},{10,11... | collective-permute-start | bytes 798728 | tf_op jit(solution)/shard_map/ppermute | solution.py:59
  220.5 67.0 %collective-permute-start.29 = (bf16[256,5120]{1,0:T(8,128)(2,1)S(1)}, bf16[256,5120]{1,0:T(8,128)(2,1)}, u32[]{:S(2)}, u32[]{:S(2)}) collective-permute-start(bf16[256,5120]{1,0:T(8,128)(2,1)S(1)} %collective-permute-done.28), channel_id=1, source_target_pairs={{0,16},{16,0},{1,17},{17,1},{2,18},{18,2},{3,19},{19,3},{4,20},{20... | collective-permute-start | bytes 7864328 | tf_op jit(solution)/shard_map/ppermute | solution.py:59
  249.4 24.4 %collective-permute-start.24 = (bf16[260,512]{1,0:T(8,128)(2,1)}, bf16[260,512]{1,0:T(8,128)(2,1)}, u32[]{:S(2)}, u32[]{:S(2)}) collective-permute-start(bf16[260,512]{1,0:T(8,128)(2,1)} %slice.134), channel_id=1, source_target_pairs={{0,1},{1,0},{2,3},{3,2},{4,5},{5,4},{6,7},{7,6},{8,9},{9,8},{10,11... | collective-permute-start | bytes 798728 | tf_op jit(solution)/shard_map/ppermute | solution.py:59
  249.8 24.0 %collective-permute-start.25 = (bf16[260,512]{1,0:T(8,128)(2,1)}, bf16[260,512]{1,0:T(8,128)(2,1)S(1)}, u32[]{:S(2)}, u32[]{:S(2)}) collective-permute-start(bf16[260,512]{1,0:T(8,128)(2,1)} %slice.135), channel_id=1, source_target_pairs={{0,1},{1,0},{2,3},{3,2},{4,5},{5,4},{6,7},{7,6},{8,9},{9,8},{10,11... | collective-permute-start | bytes 798728 | tf_op jit(solution)/shard_map/ppermute | solution.py:59
  251.0 22.8 %collective-permute-start.26 = (bf16[260,512]{1,0:T(8,128)(2,1)}, bf16[260,512]{1,0:T(8,128)(2,1)S(1)}, u32[]{:S(2)}, u32[]{:S(2)}) collective-permute-start(bf16[260,512]{1,0:T(8,128)(2,1)} %slice.136), channel_id=1, source_target_pairs={{0,1},{1,0},{2,3},{3,2},{4,5},{5,4},{6,7},{7,6},{8,9},{9,8},{10,11... | collective-permute-start | bytes 798728 | tf_op jit(solution)/shard_map/ppermute | solution.py:59
  299.6 52.8 %collective-permute-start.31 = (bf16[260,2560]{1,0:T(8,128)(2,1)}, bf16[260,2560]{1,0:T(8,128)(2,1)}, u32[]{:S(2)}, u32[]{:S(2)}) collective-permute-start(bf16[260,2560]{1,0:T(8,128)(2,1)} %project.11), channel_id=1, source_target_pairs={{0,2},{1,3},{2,0},{3,1},{4,6},{5,7},{6,4},{7,5},{8,10},{9,11},{10,... | collective-permute-start | bytes 3993608 | tf_op jit(solution)/shard_map/ppermute | solution.py:59
  315.8 74.6 %collective-permute-start.34 = (bf16[260,2560]{1,0:T(8,128)(2,1)}, bf16[260,2560]{1,0:T(8,128)(2,1)}, u32[]{:S(2)}, u32[]{:S(2)}) collective-permute-start(bf16[260,2560]{1,0:T(8,128)(2,1)} %project.15), channel_id=1, source_target_pairs={{0,2},{1,3},{2,0},{3,1},{4,6},{5,7},{6,4},{7,5},{8,10},{9,11},{10,... | collective-permute-start | bytes 3993608 | tf_op jit(solution)/shard_map/ppermute | solution.py:59
  324.4 114.3 %collective-permute-start.30 = (bf16[260,2560]{1,0:T(8,128)(2,1)}, bf16[260,2560]{1,0:T(8,128)(2,1)}, u32[]{:S(2)}, u32[]{:S(2)}) collective-permute-start(bf16[260,2560]{1,0:T(8,128)(2,1)} %project.9), channel_id=1, source_target_pairs={{0,2},{1,3},{2,0},{3,1},{4,6},{5,7},{6,4},{7,5},{8,10},{9,11},{10,... | collective-permute-start | bytes 3993608 | tf_op jit(solution)/shard_map/ppermute | solution.py:59
  334.5 133.2 %collective-permute-start.33 = (bf16[260,2560]{1,0:T(8,128)(2,1)}, bf16[260,2560]{1,0:T(8,128)(2,1)}, u32[]{:S(2)}, u32[]{:S(2)}) collective-permute-start(bf16[260,2560]{1,0:T(8,128)(2,1)} %project.13), channel_id=1, source_target_pairs={{0,2},{1,3},{2,0},{3,1},{4,6},{5,7},{6,4},{7,5},{8,10},{9,11},{10,... | collective-permute-start | bytes 3993608 | tf_op jit(solution)/shard_map/ppermute | solution.py:59
  355.4 112.3 %collective-permute-start.32 = (bf16[260,2560]{1,0:T(8,128)(2,1)}, bf16[260,2560]{1,0:T(8,128)(2,1)}, u32[]{:S(2)}, u32[]{:S(2)}) collective-permute-start(bf16[260,2560]{1,0:T(8,128)(2,1)} %add_convert_fusion.3), channel_id=1, source_target_pairs={{0,4},{1,5},{2,6},{3,7},{4,0},{5,1},{6,2},{7,3},{8,12},{9,13},{10,... | collective-permute-start | bytes 3993608 | tf_op jit(solution)/shard_map/ppermute | solution.py:59
  393.1 83.1 %collective-permute-start.35 = (bf16[260,2560]{1,0:T(8,128)(2,1)}, bf16[260,2560]{1,0:T(8,128)(2,1)}, u32[]{:S(2)}, u32[]{:S(2)}) collective-permute-start(bf16[260,2560]{1,0:T(8,128)(2,1)} %add_convert_fusion.2), channel_id=1, source_target_pairs={{0,4},{1,5},{2,6},{3,7},{4,0},{5,1},{6,2},{7,3},{8,12},{9,13},{10,... | collective-permute-start | bytes 3993608 | tf_op jit(solution)/shard_map/ppermute | solution.py:59
  (27 other events, 399.5 us)
where the time goes:
time: 528 us; the launch traced here: 525 us
  waiting for transfers between devices  205 us (39%)
  Pallas kernels  149 us (28%)
  starting transfers between devices  103 us (20%)
  local copies, waits for them, and re-layouts  45.1 us (9%)
  other arithmetic  13.8 us (3%)
  matrix products  7.19 us (1%)
    ppermute x36, waiting for transfers between devices, swap(): lax.ppermute(value, axis, [(i, i ^ flip) for i in range(lax.axis_size(axi...  176 us
    ppermute x36, starting transfers between devices, swap(): lax.ppermute(value, axis, [(i, i ^ flip) for i in range(lax.axis_size(axi...  95 us
    pallas_call x8, Pallas kernels, project(): pl.pallas_call(lambda *refs: project_kernel(len(lefts), *refs), grid=(til...  70.5 us
    pallas_call x4, Pallas kernels, attend(): pl.pallas_call(lambda *refs: attend_kernel(len(near), len(far), padded, *...  42.7 us
    pallas_call x16, Pallas kernels, turn(): pl.pallas_call(turn_kernel, grid_spec=pltpu.PrefetchScalarGridSpec(num_sc...  35.8 us
    slice x16, local copies, waits for them, and re-layouts, shards(): far.append(swap(block[:, :2 * width], 'seq', flip))  23.5 us
    ppermute x1, waiting for transfers between devices, shards(): lax.ppermute(stepped.astype(jnp.bfloat16), 'expert', [(0, 1)])[None]  20 us
  transfers between devices with their start and end apart: 40, of which 17 were waited for; matrix products, arithmetic and copies ran while one was open for 9% of the time, Pallas kernels for 27%

commit v1 on v0

--- a/solution.py
+++ b/solution.py
@@ -103,7 +103,7 @@
 def attend_kernel(near_count, far_count, padded, *refs):
     pairs = refs[: near_count + far_count]
     asking = refs[near_count + far_count : 2 * near_count + far_count]
-    out_ref, k_scr, v_scr = refs[2 * near_count + far_count :]
+    out_ref, k_scr, v_scr = refs[-3:]
     rows = pairs[0].shape[0]
 
     @pl.when(pl.program_id(0) == 0)
@@ -132,7 +132,7 @@
         out_ref[slot] = (mixed / total).astype(jnp.bfloat16)
 
 
-def attend(near, far, width):
+def attend(near, far, width, mixed, chunk):
     rows = near[0].shape[0]
     padded = -(-rows // 16) * 16
     blocks = len(near) + len(far)
@@ -143,49 +143,21 @@
         lambda *refs: attend_kernel(len(near), len(far), padded, *refs),
         grid=(heads,),
         in_specs=[pl.BlockSpec((rows, 2 * HEAD_DIM), lambda h: (0, h))] * blocks
-        + [pl.BlockSpec((rows, HEAD_DIM), lambda h: (0, 2 * heads + h))] * len(near),
-        out_specs=pl.BlockSpec((len(near), rows, HEAD_DIM), lambda h: (0, 0, h)),
-        out_shape=jax.ShapeDtypeStruct((len(near), rows, width), jnp.bfloat16),
+        + [pl.BlockSpec((rows, HEAD_DIM), lambda h: (0, 2 * heads + h))] * len(near)
+        + [pl.BlockSpec(memory_space=pl.ANY)] * (mixed is not None),
+        out_specs=pl.BlockSpec((len(near), rows, HEAD_DIM), lambda h: (0, 0, chunk * heads + h)),
+        out_shape=jax.ShapeDtypeStruct((len(near), rows, CHUNKS * width), jnp.bfloat16),
+        input_output_aliases={} if mixed is None else {2 * len(near) + len(far): 0},
         scratch_shapes=[pltpu.VMEM((keys, HEAD_DIM), jnp.bfloat16)] * 2,
         cost_estimate=pl.CostEstimate(
             flops=4 * work, bytes_accessed=8 * blocks * rows * width, transcendentals=work // HEAD_DIM
         ),
         name="attend",
-    )(*near, *far, *near)
-
-
-def project_kernel(count, *refs):
-    weight_ref, out_ref = refs[count:]
-    total, start = 0.0, 0
-    for left in refs[:count]:
-        depth = left.shape[1]
-        total += jnp.dot(
-            left[...], weight_ref[pl.ds(start, depth), :], preferred_element_type=jnp.float32
-        )
-        start += depth
-    out_ref[...] = total.astype(out_ref.dtype)
-
-
-def project(slot, chunk, lefts, weight, dtype):
-    rows = lefts[0].shape[1]
-    depth = weight.shape[0]
-    columns = weight.shape[1] // COLUMN_CHUNKS
-    tiles = 10
-    tile = columns // tiles
-    return pl.pallas_call(
-        lambda *refs: project_kernel(len(lefts), *refs),
-        grid=(tiles,),
-        in_specs=[pl.BlockSpec((None, rows, left.shape[2]), lambda t: (slot, 0, 0)) for left in lefts]
-        + [pl.BlockSpec((depth, tile), lambda t: (0, chunk * tiles + t))],
-        out_specs=pl.BlockSpec((rows, tile), lambda t: (0, t)),
-        out_shape=jax.ShapeDtypeStruct((rows, columns), dtype),
-        cost_estimate=pl.CostEstimate(
-            flops=2 * rows * depth * columns,
-            bytes_accessed=2 * depth * (columns + rows) + 4 * rows * columns,
-            transcendentals=0,
-        ),
-        name="project",
-    )(*lefts, weight)
+    )(*near, *far, *near, *([] if mixed is None else [mixed]))
+
+
+def project(block, weight, dtype):
+    return jnp.dot(block, weight, preferred_element_type=jnp.float32).astype(dtype)
 
 
 def shards(
@@ -214,8 +186,16 @@
     width = cycle_count * stored // CHUNKS
 
     own_weight = out_weight[0]
-    weight = jnp.zeros((cycle_count * stored, model_width), own_weight.dtype)
-    weight = lax.dynamic_update_slice_in_dim(weight, own_weight, cycle * stored, 0)
+    columns = model_width // COLUMN_CHUNKS
+    spans = [slice(chunk * columns, (chunk + 1) * columns) for chunk in range(COLUMN_CHUNKS)]
+    weights = [jnp.concatenate([own_weight[:, span]] * cycle_count, axis=0) for span in spans]
+
+    def put(piece, start):
+        return [
+            lax.dynamic_update_slice_in_dim(whole, piece[:, span], start, 0)
+            for whole, span in zip(weights, spans)
+        ]
+
     for flip in range(1, cycle_count):
         base = (cycle ^ flip) * stored
         if group_count % 2 == 0:
@@ -223,10 +203,10 @@
             mine = lax.dynamic_slice_in_dim(own_weight, group_bit * half, half, 0)
             first = swap(mine, "seq", flip)
             second = swap(first, "groups", 1)
-            weight = lax.dynamic_update_slice_in_dim(weight, first, base + group_bit * half, 0)
-            weight = lax.dynamic_update_slice_in_dim(weight, second, base + (1 - group_bit) * half, 0)
+            weights = put(first, base + group_bit * half)
+            weights = put(second, base + (1 - group_bit) * half)
         else:
-            weight = lax.dynamic_update_slice_in_dim(weight, swap(own_weight, "seq", flip), base, 0)
+            weights = put(swap(own_weight, "seq", flip), base)
 
     orders = lax.dynamic_index_in_dim(token_order, expert_index, 0, keepdims=False)[0]
     own_tokens = lax.dynamic_slice_in_dim(orders, seq_index * rows, rows)
@@ -236,7 +216,7 @@
     tables = (jnp.cos(angles), jnp.where(odd, 0.0, -sine), jnp.where(odd, sine, 0.0))
     place_arr = place[None].astype(jnp.int32)
 
-    mixed = []
+    mixed = None
     for chunk in range(CHUNKS):
         near, far = [], []
         for flip in (3, 2, 1, 0):
@@ -257,7 +237,7 @@
         for block in near:
             for flip in range(1, cycle_count):
                 far.append(swap(block[:, : 2 * width], "seq", flip))
-        mixed.append(attend(near, far, width))
+        mixed = attend(near, far, width, mixed, chunk)
 
     step_value = timesteps[0, 0].astype(jnp.float32)
     embedded = stamp_embedding(step_value).astype(jnp.bfloat16)
@@ -266,15 +246,15 @@
     shift_vec = modulation[model_width : 2 * model_width]
     scale_vec = modulation[2 * model_width :]
 
-    columns = model_width // COLUMN_CHUNKS
     hidden = []
     for chunk in range(COLUMN_CHUNKS):
         span = slice(chunk * columns, (chunk + 1) * columns)
-        far_sum = swap(project(3, chunk, mixed, weight, jnp.bfloat16), "seq", cycle_count)
-        near_sum = swap(project(1, chunk, mixed, weight, jnp.bfloat16), "seq", cycle_count)
-        passed = project(2, chunk, mixed, weight, jnp.float32) + far_sum.astype(jnp.float32)
+        far_sum = swap(project(mixed[3], weights[chunk], jnp.bfloat16), "seq", cycle_count)
+        near_sum = swap(project(mixed[1], weights[chunk], jnp.bfloat16), "seq", cycle_count)
+        passed = project(mixed[2], weights[chunk], jnp.float32) + far_sum.astype(jnp.float32)
         passed = swap(passed.astype(jnp.bfloat16), "seq", 2 * cycle_count)
-        kept = project(0, chunk, mixed, weight, jnp.float32) + near_sum.astype(jnp.float32)
+        kept = lax.optimization_barrier(project(mixed[0], weights[chunk], jnp.float32))
+        kept += near_sum.astype(jnp.float32)
         projected = kept + passed.astype(jnp.float32)
         hidden.append(residual[0, 0, :, span].astype(jnp.float32) + gate_vec[span] * projected)
     mean = sum(jnp.sum(part, axis=1, keepdims=True) for part in hidden) / model_width
@@ -290,19 +270,15 @@
         velocity += jnp.dot(normed, head_weight[0, span], preferred_element_type=jnp.float32)
     change = noise_level(step_value - STRIDE) - noise_level(step_value)
     stepped = latent[0] + change * velocity
-    arrived = lax.ppermute(stepped.astype(jnp.bfloat16), "expert", [(0, 1)])[None]
-    positions = seq_index[None]
-    flip = seq_count // 2
-    while flip:
-        route = [(seq_count + i, seq_count + (i ^ flip)) for i in range(seq_count)]
-        arrived = jnp.concatenate([arrived, lax.ppermute(arrived, ("expert", "seq"), route)], axis=0)
-        positions = jnp.concatenate([positions, positions ^ flip])
-        flip //= 2
+    sent = stepped.astype(jnp.bfloat16)
+    arrived = []
+    for flip in range(seq_count - 1, -1, -1):
+        route = [(i, seq_count + (i ^ flip)) for i in range(seq_count)]
+        arrived.append(lax.ppermute(sent, ("expert", "seq"), route))
+    positions = jnp.stack([seq_index ^ flip for flip in range(seq_count - 1, -1, -1)])
     first_order = token_order[0, 0].reshape(seq_count, rows)[positions].reshape(-1)
     chosen = (own_tokens[:, None] == first_order[None]).astype(jnp.bfloat16)
-    started = jnp.dot(
-        chosen, arrived.reshape(seq_count * rows, -1), preferred_element_type=jnp.float32
-    )
+    started = jnp.dot(chosen, jnp.concatenate(arrived), preferred_element_type=jnp.float32)
     finished = jnp.where(expert_index == 0, stepped, started + change * velocity)
     return (velocity[None, None], finished[None, None])
 

time: 528 us -> 513 us (0.972)
  the two profiles are of different devices: /device:TPU:1 before, /device:TPU:0 now
where the time goes in v1:
time: 513 us; the launch traced here: 506 us
  waiting for transfers between devices  249 us (49%)
  starting transfers between devices  108 us (21%)
  Pallas kernels  78.4 us (15%)
  local copies, waits for them, and re-layouts  31.6 us (6%)
  matrix products  22 us (4%)
  other arithmetic  15.5 us (3%)
    ppermute x36, waiting for transfers between devices, swap(): lax.ppermute(value, axis, [(i, i ^ flip) for i in range(lax.axis_size(axi...  249 us
    ppermute x36, starting transfers between devices, swap(): lax.ppermute(value, axis, [(i, i ^ flip) for i in range(lax.axis_size(axi...  95.8 us
    pallas_call x4, Pallas kernels, attend(): pl.pallas_call(lambda *refs: attend_kernel(len(near), len(far), padded, *...  42.6 us
    pallas_call x16, Pallas kernels, turn(): pl.pallas_call(turn_kernel, grid_spec=pltpu.PrefetchScalarGridSpec(num_sc...  35.8 us
    dot_general x8, matrix products, project(): jnp.dot(block, weight, preferred_element_type=jnp.float32).astype(dtype)  18.1 us
    slice x16, local copies, waits for them, and re-layouts, shards(): far.append(swap(block[:, :2 * width], 'seq', flip))  12.3 us
    ppermute x8, starting transfers between devices, shards(): arrived.append(lax.ppermute(sent, ('expert', 'seq'), route))  11.7 us
    concatenate x1, other arithmetic, shards(): jnp.concatenate([own_weight[:, span]] * cycle_count, axis=0)  10.5 us
  transfers between devices with their start and end apart: 44, of which 14 were waited for; matrix products, arithmetic and copies ran while one was open for 9% of the time, Pallas kernels for 15%

profile of v1, /device:TPU:0, one launch (start us, length us, event | category | flops | bytes accessed | tf_op | source)
XLA Modules:
  0.0 506.4 jit_solution(12384530418331552457)
XLA Ops:
  0.6 3.4 dynamic-slice_bitcast_fusion
  4.0 3.0 collective-permute-start.28
  34.8 36.0 %collective-permute-done.10.refs_4_ = bf16[260,512]{1,0:T(8,128)(2,1)} collective-permute-done((bf16[260,512]{1,0:T(8,128)(2,1)S(1)}, bf16[260,512]{1,0:T(8,128)(2,1)}, u32[]{:S(2)}, u32[]{:S(2)}) %collective-permute-start.10) | collective-permute-done | bytes 266272 | tf_op jit(solution)/shard_map/ppermute | solution.py:59
  70.8 3.1 collective-permute-start.1
  73.9 2.7 collective-permute-done.17.refs_4_
  76.6 4.1 collective-permute-start.2
  83.4 2.6 collective-permute-start.8
  95.0 7.7 %collective-permute-done.1.refs_2_.refs_10_ = bf16[260,768]{1,0:T(8,128)(2,1)S(1)} collective-permute-done((bf16[260,768]{1,0:T(8,128)(2,1)S(1)}, bf16[260,768]{1,0:T(8,128)(2,1)S(1)}, u32[]{:S(2)}, u32[]{:S(2)}) %collective-permute-start.1) | collective-permute-done | bytes 399392 | tf_op jit(solution)/shard_map/ppermute | solution.py:59
  104.1 22.4 %collective-permute-start.21 = (bf16[260,768]{1,0:T(8,128)(2,1)}, bf16[260,768]{1,0:T(8,128)(2,1)}, u32[]{:S(2)}, u32[]{:S(2)}) collective-permute-start(bf16[260,768]{1,0:T(8,128)(2,1)} %turn.29), channel_id=1, source_target_pairs={{0,2},{1,3},{2,0},{3,1},{4,6},{5,7},{6,4},{7,5},{8,10},{9,11},{10,... | collective-permute-start | bytes 1198088 | tf_op jit(solution)/shard_map/ppermute | solution.py:59
  127.6 7.1 %collective-permute-done.8.refs_2_.refs_10_ = bf16[260,768]{1,0:T(8,128)(2,1)S(1)} collective-permute-done((bf16[260,768]{1,0:T(8,128)(2,1)}, bf16[260,768]{1,0:T(8,128)(2,1)S(1)}, u32[]{:S(2)}, u32[]{:S(2)}) %collective-permute-start.8) | collective-permute-done | bytes 399392 | tf_op jit(solution)/shard_map/ppermute | solution.py:59
  144.0 17.3 %collective-permute-start.14 = (bf16[260,768]{1,0:T(8,128)(2,1)}, bf16[260,768]{1,0:T(8,128)(2,1)S(1)}, u32[]{:S(2)}, u32[]{:S(2)}) collective-permute-start(bf16[260,768]{1,0:T(8,128)(2,1)} %turn.25), channel_id=1, source_target_pairs={{0,2},{1,3},{2,0},{3,1},{4,6},{5,7},{6,4},{7,5},{8,10},{9,11},{10,... | collective-permute-start | bytes 1198088 | tf_op jit(solution)/shard_map/ppermute | solution.py:59
  162.4 7.2 %collective-permute-done.22.refs_2_.refs_10_ = bf16[260,768]{1,0:T(8,128)(2,1)} collective-permute-done((bf16[260,768]{1,0:T(8,128)(2,1)S(1)}, bf16[260,768]{1,0:T(8,128)(2,1)}, u32[]{:S(2)}, u32[]{:S(2)}) %collective-permute-start.22) | collective-permute-done | bytes 399392 | tf_op jit(solution)/shard_map/ppermute | solution.py:59
  169.6 2.5 collective-permute-start.16
  173.7 2.9 fusion.38
  180.5 23.8 %collective-permute-done.15.refs_2_.refs_10_ = bf16[260,768]{1,0:T(8,128)(2,1)S(1)} collective-permute-done((bf16[260,768]{1,0:T(8,128)(2,1)}, bf16[260,768]{1,0:T(8,128)(2,1)S(1)}, u32[]{:S(2)}, u32[]{:S(2)}) %collective-permute-start.15) | collective-permute-done | bytes 399392 | tf_op jit(solution)/shard_map/ppermute | solution.py:59
  209.3 10.5 %pad_maximum_fusion = (bf16[1024,2560]{1,0:T(8,128)(2,1)}, bf16[1024,2560]{1,0:T(8,128)(2,1)}) fusion(bf16[512,2560]{1,0:T(8,128)(2,1)S(1)} %get-tuple-element.8, bf16[512,2560]{1,0:T(8,128)(2,1)S(1)} %get-tuple-element.9), kind=kLoop, calls=%fused_computation.3 | loop fusion | flops 20971520 | bytes 15728640 | tf_op jit(solution)/shard_map/concatenate | solution.py:191
  234.4 10.6 %attend.4.refs_12_ = bf16[4,260,1024]{2,1,0:T(8,128)(2,1)} custom-call(bf16[260,768]{1,0:T(8,128)(2,1)} %turn.28.refs_0_.refs_8_, bf16[260,768]{1,0:T(8,128)(2,1)} %collective-permute-done.21.refs_1_.refs_9_, bf16[260,768]{1,0:T(8,128)(2,1)} %collective-permute-done.22.refs_2_.refs_10_, bf16[260,768]{1,0:T(8,128)(2,1)} %collective-permute-done.23.refs_3_.refs_11_, ...), custom_call_target="tpu_custom_call" | custom-call | flops 2317352960 | bytes 4259840 | tf_op jit(solution)/shard_map/attend/pallas_call | solution.py:142
  249.7 10.8 %attend.5.refs_12_ = bf16[4,260,1024]{2,1,0:T(8,128)(2,1)} custom-call(bf16[260,768]{1,0:T(8,128)(2,1)} %turn.24.refs_0_.refs_8_, bf16[260,768]{1,0:T(8,128)(2,1)} %copy-done.7, bf16[260,768]{1,0:T(8,128)(2,1)} %copy-done.8, bf16[260,768]{1,0:T(8,128)(2,1)} %copy-done.9, ...), custom_call_target="tpu_custom_call", output_to_operand_aliasing={{}: (12, {})} | custom-call | flops 2317352960 | bytes 4259840 | tf_op jit(solution)/shard_map/attend/pallas_call | solution.py:142
  260.4 10.6 %attend.6.refs_12_ = bf16[4,260,1024]{2,1,0:T(8,128)(2,1)} custom-call(bf16[260,768]{1,0:T(8,128)(2,1)} %turn.20.refs_0_.refs_8_, bf16[260,768]{1,0:T(8,128)(2,1)} %copy-done.4, bf16[260,768]{1,0:T(8,128)(2,1)} %copy-done.5, bf16[260,768]{1,0:T(8,128)(2,1)} %copy-done.6, ...), custom_call_target="tpu_custom_call", output_to_operand_aliasing={{}: (12, {})} | custom-call | flops 2317352960 | bytes 4259840 | tf_op jit(solution)/shard_map/attend/pallas_call | solution.py:142
  272.6 10.7 %attend.7 = bf16[4,260,1024]{2,1,0:T(8,128)(2,1)} custom-call(bf16[260,768]{1,0:T(8,128)(2,1)} %turn.16.refs_0_.refs_8_, bf16[260,768]{1,0:T(8,128)(2,1)} %copy-done.1, bf16[260,768]{1,0:T(8,128)(2,1)} %copy-done.2, bf16[260,768]{1,0:T(8,128)(2,1)} %copy-done.3, bf16[260,512]{1,0:T(8,128)(2,1)} %copy-done.20, ...), custom_call_target="tpu_custom_call", output_to_operand_aliasing={{}: (12, {})} | custom-call | flops 2317352960 | bytes 4259840 | tf_op jit(solution)/shard_map/attend/pallas_call | solution.py:142
  283.4 3.4 slice_dynamic-update-slice_fusion.3
  286.8 3.6 slice_dynamic-update-slice_fusion.2
  290.4 4.2 convolution_convert_fusion.2
  294.6 9.2 %collective-permute-start.31 = (bf16[260,2560]{1,0:T(8,128)(2,1)S(1)}, bf16[260,2560]{1,0:T(8,128)(2,1)S(1)}, u32[]{:S(2)}, u32[]{:S(2)}) collective-permute-start(bf16[260,2560]{1,0:T(8,128)(2,1)S(1)} %convolution_convert_fusion.2), channel_id=1, source_target_pairs={{0,2},{1,3},{2,0},{3,1},{4,6},{5,7},{6,4},{7,5},{8,10},{9,11},{10,... | collective-permute-start | bytes 3993608 | tf_op jit(solution)/shard_map/ppermute | solution.py:59
  303.8 4.2 convolution_convert_fusion
  313.5 35.3 %collective-permute-done.31 = bf16[260,2560]{1,0:T(8,128)(2,1)S(1)} collective-permute-done((bf16[260,2560]{1,0:T(8,128)(2,1)S(1)}, bf16[260,2560]{1,0:T(8,128)(2,1)S(1)}, u32[]{:S(2)}, u32[]{:S(2)}) %collective-permute-start.31) | collective-permute-done | bytes 1331232 | tf_op jit(solution)/shard_map/ppermute | solution.py:59
  351.8 54.9 %collective-permute-done.34 = bf16[260,2560]{1,0:T(8,128)(2,1)S(1)} collective-permute-done((bf16[260,2560]{1,0:T(8,128)(2,1)S(1)}, bf16[260,2560]{1,0:T(8,128)(2,1)S(1)}, u32[]{:S(2)}, u32[]{:S(2)}) %collective-permute-start.34) | collective-permute-done | bytes 1331232 | tf_op jit(solution)/shard_map/ppermute | solution.py:59
  413.0 29.7 %collective-permute-done.30 = bf16[260,2560]{1,0:T(8,128)(2,1)S(1)} collective-permute-done((bf16[260,2560]{1,0:T(8,128)(2,1)S(1)}, bf16[260,2560]{1,0:T(8,128)(2,1)S(1)}, u32[]{:S(2)}, u32[]{:S(2)}) %collective-permute-start.30) | collective-permute-done | bytes 1331232 | tf_op jit(solution)/shard_map/ppermute | solution.py:59
  442.7 24.6 %collective-permute-done.33 = bf16[260,2560]{1,0:T(8,128)(2,1)S(1)} collective-permute-done((bf16[260,2560]{1,0:T(8,128)(2,1)S(1)}, bf16[260,2560]{1,0:T(8,128)(2,1)S(1)}, u32[]{:S(2)}, u32[]{:S(2)}) %collective-permute-start.33) | collective-permute-done | bytes 1331232 | tf_op jit(solution)/shard_map/ppermute | solution.py:59
  467.3 18.0 %collective-permute-done.35 = bf16[260,2560]{1,0:T(8,128)(2,1)S(1)} collective-permute-done((bf16[260,2560]{1,0:T(8,128)(2,1)S(1)}, bf16[260,2560]{1,0:T(8,128)(2,1)S(1)}, u32[]{:S(2)}, u32[]{:S(2)}) %collective-permute-start.35) | collective-permute-done | bytes 1331232 | tf_op jit(solution)/shard_map/ppermute | solution.py:59
  486.4 2.9 fusion.37
  499.9 2.6 collective-permute-start.42
  (217 shorter events, 112.6 us)
Async XLA Ops:
  4.0 203.8 %collective-permute-start.28 = (bf16[256,5120]{1,0:T(8,128)(2,1)}, bf16[256,5120]{1,0:T(8,128)(2,1)}, u32[]{:S(2)}, u32[]{:S(2)}) collective-permute-start(bf16[256,5120]{1,0:T(8,128)(2,1)} %dynamic-slice_bitcast_fusion), channel_id=1, source_target_pairs={{0,1},{1,0},{2,3},{3,2},{4,5},{5,4},{6,7},{7,6},{8,9},{9,8},{10,11... | collective-permute-start | bytes 7864328 | tf_op jit(solution)/shard_map/ppermute | solution.py:59
  12.0 71.4 %collective-permute-start = (bf16[260,768]{1,0:T(8,128)(2,1)}, bf16[260,768]{1,0:T(8,128)(2,1)S(1)}, u32[]{:S(2)}, u32[]{:S(2)}) collective-permute-start(bf16[260,768]{1,0:T(8,128)(2,1)} %turn.17), channel_id=1, source_target_pairs={{0,2},{1,3},{2,0},{3,1},{4,6},{5,7},{6,4},{7,5},{8,10},{9,11},{10,... | collective-permute-start | bytes 1198088 | tf_op jit(solution)/shard_map/ppermute | solution.py:59
  16.7 54.1 %collective-permute-start.10 = (bf16[260,512]{1,0:T(8,128)(2,1)S(1)}, bf16[260,512]{1,0:T(8,128)(2,1)}, u32[]{:S(2)}, u32[]{:S(2)}) collective-permute-start(bf16[260,512]{1,0:T(8,128)(2,1)S(1)} %slice.170), channel_id=1, source_target_pairs={{0,1},{1,0},{2,3},{3,2},{4,5},{5,4},{6,7},{7,6},{8,9},{9,8},{10,11... | collective-permute-start | bytes 798728 | tf_op jit(solution)/shard_map/ppermute | solution.py:59
  20.5 56.1 %collective-permute-start.17 = (bf16[260,512]{1,0:T(8,128)(2,1)S(1)}, bf16[260,512]{1,0:T(8,128)(2,1)}, u32[]{:S(2)}, u32[]{:S(2)}) collective-permute-start(bf16[260,512]{1,0:T(8,128)(2,1)S(1)} %slice.174), channel_id=1, source_target_pairs={{0,1},{1,0},{2,3},{3,2},{4,5},{5,4},{6,7},{7,6},{8,9},{9,8},{10,11... | collective-permute-start | bytes 798728 | tf_op jit(solution)/shard_map/ppermute | solution.py:59
  25.3 56.3 %collective-permute-start.24 = (bf16[260,512]{1,0:T(8,128)(2,1)S(1)}, bf16[260,512]{1,0:T(8,128)(2,1)}, u32[]{:S(2)}, u32[]{:S(2)}) collective-permute-start(bf16[260,512]{1,0:T(8,128)(2,1)S(1)} %slice.178), channel_id=1, source_target_pairs={{0,1},{1,0},{2,3},{3,2},{4,5},{5,4},{6,7},{7,6},{8,9},{9,8},{10,11... | collective-permute-start | bytes 798728 | tf_op jit(solution)/shard_map/ppermute | solution.py:59
  70.8 31.9 %collective-permute-start.1 = (bf16[260,768]{1,0:T(8,128)(2,1)S(1)}, bf16[260,768]{1,0:T(8,128)(2,1)S(1)}, u32[]{:S(2)}, u32[]{:S(2)}) collective-permute-start(bf16[260,768]{1,0:T(8,128)(2,1)S(1)} %copy-done.14), channel_id=1, source_target_pairs={{0,4},{1,5},{2,6},{3,7},{4,0},{5,1},{6,2},{7,3},{8,12},{9,13},{10,... | collective-permute-start | bytes 1198088 | tf_op jit(solution)/shard_map/ppermute | solution.py:59
  76.6 27.5 %collective-permute-start.2 = (bf16[260,768]{1,0:T(8,128)(2,1)}, bf16[260,768]{1,0:T(8,128)(2,1)S(1)}, u32[]{:S(2)}, u32[]{:S(2)}) collective-permute-start(bf16[260,768]{1,0:T(8,128)(2,1)} %turn.19), channel_id=1, source_target_pairs={{0,6},{1,7},{2,4},{3,5},{4,2},{5,3},{6,0},{7,1},{8,14},{9,15},{10,... | collective-permute-start | bytes 1198088 | tf_op jit(solution)/shard_map/ppermute | solution.py:59
  81.6 45.0 %collective-permute-start.7 = (bf16[260,768]{1,0:T(8,128)(2,1)S(1)}, bf16[260,768]{1,0:T(8,128)(2,1)S(1)}, u32[]{:S(2)}, u32[]{:S(2)}) collective-permute-start(bf16[260,768]{1,0:T(8,128)(2,1)S(1)} %copy-done.12), channel_id=1, source_target_pairs={{0,2},{1,3},{2,0},{3,1},{4,6},{5,7},{6,4},{7,5},{8,10},{9,11},{10,... | collective-permute-start | bytes 1198088 | tf_op jit(solution)/shard_map/ppermute | solution.py:59
  83.4 51.3 %collective-permute-start.8 = (bf16[260,768]{1,0:T(8,128)(2,1)}, bf16[260,768]{1,0:T(8,128)(2,1)S(1)}, u32[]{:S(2)}, u32[]{:S(2)}) collective-permute-start(bf16[260,768]{1,0:T(8,128)(2,1)} %turn.22), channel_id=1, source_target_pairs={{0,4},{1,5},{2,6},{3,7},{4,0},{5,1},{6,2},{7,3},{8,12},{9,13},{10,... | collective-permute-start | bytes 1198088 | tf_op jit(solution)/shard_map/ppermute | solution.py:59
  102.7 41.3 %collective-permute-start.9 = (bf16[260,768]{1,0:T(8,128)(2,1)}, bf16[260,768]{1,0:T(8,128)(2,1)S(1)}, u32[]{:S(2)}, u32[]{:S(2)}) collective-permute-start(bf16[260,768]{1,0:T(8,128)(2,1)} %turn.23), channel_id=1, source_target_pairs={{0,6},{1,7},{2,4},{3,5},{4,2},{5,3},{6,0},{7,1},{8,14},{9,15},{10,... | collective-permute-start | bytes 1198088 | tf_op jit(solution)/shard_map/ppermute | solution.py:59
  104.1 57.2 %collective-permute-start.21 = (bf16[260,768]{1,0:T(8,128)(2,1)}, bf16[260,768]{1,0:T(8,128)(2,1)}, u32[]{:S(2)}, u32[]{:S(2)}) collective-permute-start(bf16[260,768]{1,0:T(8,128)(2,1)} %turn.29), channel_id=1, source_target_pairs={{0,2},{1,3},{2,0},{3,1},{4,6},{5,7},{6,4},{7,5},{8,10},{9,11},{10,... | collective-permute-start | bytes 1198088 | tf_op jit(solution)/shard_map/ppermute | solution.py:59
  126.6 43.1 %collective-permute-start.22 = (bf16[260,768]{1,0:T(8,128)(2,1)S(1)}, bf16[260,768]{1,0:T(8,128)(2,1)}, u32[]{:S(2)}, u32[]{:S(2)}) collective-permute-start(bf16[260,768]{1,0:T(8,128)(2,1)S(1)} %copy-done.13), channel_id=1, source_target_pairs={{0,4},{1,5},{2,6},{3,7},{4,0},{5,1},{6,2},{7,3},{8,12},{9,13},{10,... | collective-permute-start | bytes 1198088 | tf_op jit(solution)/shard_map/ppermute | solution.py:59
  134.7 37.5 %collective-permute-start.23 = (bf16[260,768]{1,0:T(8,128)(2,1)}, bf16[260,768]{1,0:T(8,128)(2,1)}, u32[]{:S(2)}, u32[]{:S(2)}) collective-permute-start(bf16[260,768]{1,0:T(8,128)(2,1)} %turn.31), channel_id=1, source_target_pairs={{0,6},{1,7},{2,4},{3,5},{4,2},{5,3},{6,0},{7,1},{8,14},{9,15},{10,... | collective-permute-start | bytes 1198088 | tf_op jit(solution)/shard_map/ppermute | solution.py:59
  144.0 35.9 %collective-permute-start.14 = (bf16[260,768]{1,0:T(8,128)(2,1)}, bf16[260,768]{1,0:T(8,128)(2,1)S(1)}, u32[]{:S(2)}, u32[]{:S(2)}) collective-permute-start(bf16[260,768]{1,0:T(8,128)(2,1)} %turn.25), channel_id=1, source_target_pairs={{0,2},{1,3},{2,0},{3,1},{4,6},{5,7},{6,4},{7,5},{8,10},{9,11},{10,... | collective-permute-start | bytes 1198088 | tf_op jit(solution)/shard_map/ppermute | solution.py:59
  161.3 42.9 %collective-permute-start.15 = (bf16[260,768]{1,0:T(8,128)(2,1)}, bf16[260,768]{1,0:T(8,128)(2,1)S(1)}, u32[]{:S(2)}, u32[]{:S(2)}) collective-permute-start(bf16[260,768]{1,0:T(8,128)(2,1)} %turn.26), channel_id=1, source_target_pairs={{0,4},{1,5},{2,6},{3,7},{4,0},{5,1},{6,2},{7,3},{8,12},{9,13},{10,... | collective-permute-start | bytes 1198088 | tf_op jit(solution)/shard_map/ppermute | solution.py:59
  169.6 36.2 %collective-permute-start.16 = (bf16[260,768]{1,0:T(8,128)(2,1)}, bf16[260,768]{1,0:T(8,128)(2,1)S(1)}, u32[]{:S(2)}, u32[]{:S(2)}) collective-permute-start(bf16[260,768]{1,0:T(8,128)(2,1)} %turn.27), channel_id=1, source_target_pairs={{0,6},{1,7},{2,4},{3,5},{4,2},{5,3},{6,0},{7,1},{8,14},{9,15},{10,... | collective-permute-start | bytes 1198088 | tf_op jit(solution)/shard_map/ppermute | solution.py:59
  172.2 34.1 %collective-permute-start.11 = (bf16[260,512]{1,0:T(8,128)(2,1)S(1)}, bf16[260,512]{1,0:T(8,128)(2,1)}, u32[]{:S(2)}, u32[]{:S(2)}) collective-permute-start(bf16[260,512]{1,0:T(8,128)(2,1)S(1)} %slice.171), channel_id=1, source_target_pairs={{0,1},{1,0},{2,3},{3,2},{4,5},{5,4},{6,7},{7,6},{8,9},{9,8},{10,11... | collective-permute-start | bytes 798728 | tf_op jit(solution)/shard_map/ppermute | solution.py:59
  179.9 43.6 %collective-permute-start.12 = (bf16[260,512]{1,0:T(8,128)(2,1)S(1)}, bf16[260,512]{1,0:T(8,128)(2,1)S(1)}, u32[]{:S(2)}, u32[]{:S(2)}) collective-permute-start(bf16[260,512]{1,0:T(8,128)(2,1)S(1)} %slice.172), channel_id=1, source_target_pairs={{0,1},{1,0},{2,3},{3,2},{4,5},{5,4},{6,7},{7,6},{8,9},{9,8},{10,11... | collective-permute-start | bytes 798728 | tf_op jit(solution)/shard_map/ppermute | solution.py:59
  207.8 78.9 %collective-permute-start.29 = (bf16[256,5120]{1,0:T(8,128)(2,1)}, bf16[256,5120]{1,0:T(8,128)(2,1)}, u32[]{:S(2)}, u32[]{:S(2)}) collective-permute-start(bf16[256,5120]{1,0:T(8,128)(2,1)} %collective-permute-done.28), channel_id=1, source_target_pairs={{0,16},{16,0},{1,17},{17,1},{2,18},{18,2},{3,19},{19,3},{4,20},{20... | collective-permute-start | bytes 7864328 | tf_op jit(solution)/shard_map/ppermute | solution.py:59
  224.0 21.7 %collective-permute-start.18 = (bf16[260,512]{1,0:T(8,128)(2,1)}, bf16[260,512]{1,0:T(8,128)(2,1)S(1)}, u32[]{:S(2)}, u32[]{:S(2)}) collective-permute-start(bf16[260,512]{1,0:T(8,128)(2,1)} %slice.175), channel_id=1, source_target_pairs={{0,1},{1,0},{2,3},{3,2},{4,5},{5,4},{6,7},{7,6},{8,9},{9,8},{10,11... | collective-permute-start | bytes 798728 | tf_op jit(solution)/shard_map/ppermute | solution.py:59
  225.5 21.6 %collective-permute-start.19 = (bf16[260,512]{1,0:T(8,128)(2,1)}, bf16[260,512]{1,0:T(8,128)(2,1)S(1)}, u32[]{:S(2)}, u32[]{:S(2)}) collective-permute-start(bf16[260,512]{1,0:T(8,128)(2,1)} %slice.176), channel_id=1, source_target_pairs={{0,1},{1,0},{2,3},{3,2},{4,5},{5,4},{6,7},{7,6},{8,9},{9,8},{10,11... | collective-permute-start | bytes 798728 | tf_op jit(solution)/shard_map/ppermute | solution.py:59
  226.0 22.9 %collective-permute-start.20 = (bf16[260,512]{1,0:T(8,128)(2,1)}, bf16[260,512]{1,0:T(8,128)(2,1)S(1)}, u32[]{:S(2)}, u32[]{:S(2)}) collective-permute-start(bf16[260,512]{1,0:T(8,128)(2,1)} %slice.177), channel_id=1, source_target_pairs={{0,1},{1,0},{2,3},{3,2},{4,5},{5,4},{6,7},{7,6},{8,9},{9,8},{10,11... | collective-permute-start | bytes 798728 | tf_op jit(solution)/shard_map/ppermute | solution.py:59
  245.0 26.0 %collective-permute-start.3 = (bf16[260,512]{1,0:T(8,128)(2,1)}, bf16[260,512]{1,0:T(8,128)(2,1)S(1)}, u32[]{:S(2)}, u32[]{:S(2)}) collective-permute-start(bf16[260,512]{1,0:T(8,128)(2,1)} %slice.166), channel_id=1, source_target_pairs={{0,1},{1,0},{2,3},{3,2},{4,5},{5,4},{6,7},{7,6},{8,9},{9,8},{10,11... | collective-permute-start | bytes 798728 | tf_op jit(solution)/shard_map/ppermute | solution.py:59
  245.7 25.3 %collective-permute-start.4 = (bf16[260,512]{1,0:T(8,128)(2,1)}, bf16[260,512]{1,0:T(8,128)(2,1)S(1)}, u32[]{:S(2)}, u32[]{:S(2)}) collective-permute-start(bf16[260,512]{1,0:T(8,128)(2,1)} %slice.167), channel_id=1, source_target_pairs={{0,1},{1,0},{2,3},{3,2},{4,5},{5,4},{6,7},{7,6},{8,9},{9,8},{10,11... | collective-permute-start | bytes 798728 | tf_op jit(solution)/shard_map/ppermute | solution.py:59
  247.1 24.0 %collective-permute-start.5 = (bf16[260,512]{1,0:T(8,128)(2,1)}, bf16[260,512]{1,0:T(8,128)(2,1)S(1)}, u32[]{:S(2)}, u32[]{:S(2)}) collective-permute-start(bf16[260,512]{1,0:T(8,128)(2,1)} %slice.168), channel_id=1, source_target_pairs={{0,1},{1,0},{2,3},{3,2},{4,5},{5,4},{6,7},{7,6},{8,9},{9,8},{10,11... | collective-permute-start | bytes 798728 | tf_op jit(solution)/shard_map/ppermute | solution.py:59
  249.0 22.1 %collective-permute-start.6 = (bf16[260,512]{1,0:T(8,128)(2,1)S(1)}, bf16[260,512]{1,0:T(8,128)(2,1)S(1)}, u32[]{:S(2)}, u32[]{:S(2)}) collective-permute-start(bf16[260,512]{1,0:T(8,128)(2,1)S(1)} %slice.169), channel_id=1, source_target_pairs={{0,1},{1,0},{2,3},{3,2},{4,5},{5,4},{6,7},{7,6},{8,9},{9,8},{10,11... | collective-permute-start | bytes 798728 | tf_op jit(solution)/shard_map/ppermute | solution.py:59
  294.6 54.2 %collective-permute-start.31 = (bf16[260,2560]{1,0:T(8,128)(2,1)S(1)}, bf16[260,2560]{1,0:T(8,128)(2,1)S(1)}, u32[]{:S(2)}, u32[]{:S(2)}) collective-permute-start(bf16[260,2560]{1,0:T(8,128)(2,1)S(1)} %convolution_convert_fusion.2), channel_id=1, source_target_pairs={{0,2},{1,3},{2,0},{3,1},{4,6},{5,7},{6,4},{7,5},{8,10},{9,11},{10,... | collective-permute-start | bytes 3993608 | tf_op jit(solution)/shard_map/ppermute | solution.py:59
  308.0 98.7 %collective-permute-start.34 = (bf16[260,2560]{1,0:T(8,128)(2,1)S(1)}, bf16[260,2560]{1,0:T(8,128)(2,1)S(1)}, u32[]{:S(2)}, u32[]{:S(2)}) collective-permute-start(bf16[260,2560]{1,0:T(8,128)(2,1)S(1)} %convolution_convert_fusion), channel_id=1, source_target_pairs={{0,2},{1,3},{2,0},{3,1},{4,6},{5,7},{6,4},{7,5},{8,10},{9,11},{10,... | collective-permute-start | bytes 3993608 | tf_op jit(solution)/shard_map/ppermute | solution.py:59
  309.7 133.0 %collective-permute-start.30 = (bf16[260,2560]{1,0:T(8,128)(2,1)S(1)}, bf16[260,2560]{1,0:T(8,128)(2,1)S(1)}, u32[]{:S(2)}, u32[]{:S(2)}) collective-permute-start(bf16[260,2560]{1,0:T(8,128)(2,1)S(1)} %convolution_convert_fusion.3), channel_id=1, source_target_pairs={{0,2},{1,3},{2,0},{3,1},{4,6},{5,7},{6,4},{7,5},{8,10},{9,11},{10,... | collective-permute-start | bytes 3993608 | tf_op jit(solution)/shard_map/ppermute | solution.py:59
  313.4 153.9 %collective-permute-start.33 = (bf16[260,2560]{1,0:T(8,128)(2,1)S(1)}, bf16[260,2560]{1,0:T(8,128)(2,1)S(1)}, u32[]{:S(2)}, u32[]{:S(2)}) collective-permute-start(bf16[260,2560]{1,0:T(8,128)(2,1)S(1)} %convolution_convert_fusion.1), channel_id=1, source_target_pairs={{0,2},{1,3},{2,0},{3,1},{4,6},{5,7},{6,4},{7,5},{8,10},{9,11},{10,... | collective-permute-start | bytes 3993608 | tf_op jit(solution)/shard_map/ppermute | solution.py:59
  350.4 116.9 %collective-permute-start.32 = (bf16[260,2560]{1,0:T(8,128)(2,1)S(1)}, bf16[260,2560]{1,0:T(8,128)(2,1)S(1)}, u32[]{:S(2)}, u32[]{:S(2)}) collective-permute-start(bf16[260,2560]{1,0:T(8,128)(2,1)S(1)} %fusion.2), channel_id=1, source_target_pairs={{0,4},{1,5},{2,6},{3,7},{4,0},{5,1},{6,2},{7,3},{8,12},{9,13},{10,... | collective-permute-start | bytes 3993608 | tf_op jit(solution)/shard_map/ppermute | solution.py:59
  408.3 77.0 %collective-permute-start.35 = (bf16[260,2560]{1,0:T(8,128)(2,1)S(1)}, bf16[260,2560]{1,0:T(8,128)(2,1)S(1)}, u32[]{:S(2)}, u32[]{:S(2)}) collective-permute-start(bf16[260,2560]{1,0:T(8,128)(2,1)S(1)} %fusion.3), channel_id=1, source_target_pairs={{0,4},{1,5},{2,6},{3,7},{4,0},{5,1},{6,2},{7,3},{8,12},{9,13},{10,... | collective-permute-start | bytes 3993608 | tf_op jit(solution)/shard_map/ppermute | solution.py:59
  (49 other events, 1125.4 us)
